TPU v7x, 32 devices: a whole 2x2x4 slice. The times are simulated.
32 devices in a mesh: phase: 2 (over core), tok: 4 (over z), mp: 4 (over y, x).
Axes of the slice: x: 2, y: 2, z: 4, core: 2. Of those that a mesh axis runs over, the one named last changes fastest.
Arguments:
- hidden: bfloat16 [2, 512, 6656], P('phase', 'tok', 'mp'), may hold values from -30 to 30
- w_qkv: bfloat16 [2, 6656, 3, 4096], P('phase', 'mp', None, 'tok'), may hold values from -1 to 1
- segment_ids: int32 [2, 512], P('phase'), may hold values from 0 to 3, never falling along the last dimension, each value on 1 to 256 neighbouring positions
- exit_flags: int32 [2, 4], P('phase'), may hold values from 0 to 1, as said below
Outputs:
- attended: bfloat16 [2, 512, 4096], P('phase', 'mp', 'tok')
- handed: bfloat16 [2, 512, 4096], P('phase', 'mp', 'tok')
Inputs may be any that keep to these rules, and one draw needn't show every extreme that they name: `exit_flags`: in each micro-batch exactly 2 of the 4 blocks have flag 0.
All inputs are finite; a program needn't handle non-finite values.
Results may differ from a plain program's by a relative error of at most 0.0068.
Values may be sent and summed in bfloat16 or wider, within the bound.
A program may use at most 64 MiB of HBM per device.

v0:
```python
import math
import jax
import jax.numpy as jnp
from jax import lax
from jax.sharding import PartitionSpec as P

HEAD = 128
BLOCK = 128


def shifted(block, axis, distance):
    devices = range(lax.axis_size(axis))
    route = [((i - distance) % len(devices), i) for i in devices]
    return lax.ppermute(block, axis, route)


def attend(query, keys, values, query_pos, segment, key_pos):
    heads_here = query.shape[1] // HEAD
    total = keys.shape[0]
    key_heads = keys.reshape(total, heads_here, HEAD)
    value_heads = values.reshape(total, heads_here, HEAD)
    key_segment = jnp.take(segment, key_pos)
    scale = 1.0 / math.sqrt(HEAD)
    block_rows = query.shape[0]
    scores = (
        jnp.einsum(
            "rhd,shd->hrs",
            query.reshape(block_rows, heads_here, HEAD),
            key_heads,
            preferred_element_type=jnp.float32,
        )
        * scale
    )
    own_segment = jnp.take(segment, query_pos)
    allowed = (key_pos[None, :] <= query_pos[:, None]) & (
        key_segment[None, :] == own_segment[:, None]
    )
    scores = jnp.where(allowed[None], scores, -1e30)
    peak = jnp.max(scores, axis=-1, keepdims=True)
    expo = jnp.exp(scores - peak)
    probs = (expo / jnp.sum(expo, axis=-1, keepdims=True)).astype(jnp.bfloat16)
    mixed = jnp.einsum("hrs,shd->rhd", probs, value_heads, preferred_element_type=jnp.float32)
    return mixed.reshape(block_rows, heads_here * HEAD).astype(jnp.bfloat16)


def local(hidden, w_qkv, segment_ids, exit_flags):
    rows_here = hidden[0]
    weights = w_qkv[0]
    width_here = rows_here.shape[1]
    head_cols = weights.shape[2]
    flat_weights = weights.reshape(width_here, 3 * head_cols)
    segment = segment_ids[0]
    flags = exit_flags[0]
    groups = lax.axis_size("mp")
    member = lax.axis_index("mp")
    partial_value = jnp.dot(
        lax.all_gather(rows_here, "tok", axis=0, tiled=True),
        flat_weights,
        preferred_element_type=jnp.float32,
    )
    total = partial_value.shape[0]
    quarter = total // groups
    query_part = partial_value[:, :head_cols]
    key_value_part = partial_value[:, head_cols:]
    my_pos = member * quarter + jnp.arange(quarter, dtype=jnp.int32)
    my_blocks = my_pos // BLOCK
    alive = jnp.take(flags, my_blocks) == 0
    query = lax.psum_scatter(query_part, "mp", scatter_dimension=0, tiled=True).astype(jnp.bfloat16)
    mine = lax.psum_scatter(key_value_part, "mp", scatter_dimension=0, tiled=True).astype(
        jnp.bfloat16
    )
    key_value = lax.all_gather(mine, "mp", axis=0, tiled=True)
    all_pos = jnp.arange(total, dtype=jnp.int32)
    mixed = attend(
        query, key_value[:, :head_cols], key_value[:, head_cols:], my_pos, segment, all_pos
    )
    zeros = jnp.zeros((quarter, head_cols), jnp.bfloat16)
    result = jnp.where(alive[:, None], mixed, zeros)
    handed = shifted(result, "phase", 1)
    return (result[None], handed[None])


def solution(mesh):
    in_specs = (
        P("phase", "tok", "mp"),
        P("phase", "mp", None, "tok"),
        P("phase", None),
        P("phase", None),
    )
    out_specs = (P("phase", "mp", "tok"), P("phase", "mp", "tok"))
    return jax.shard_map(local, mesh=mesh, in_specs=in_specs, out_specs=out_specs, check_vma=False)
```

profile of v0, /device:TPU:0, one launch (start us, length us, event | category | flops | bytes accessed | tf_op | source)
XLA Modules:
  0.0 207.5 jit_solution(11496909522336261351)
XLA Ops:
  7.2 0.7 all-gather.6.cloned.1.call-update
  8.0 13.5 %copy.11 = bf16[1,1664,3,1024]{1,3,2,0:T(8,128)(2,1)} copy(bf16[1,1664,3,1024]{3,1,2,0:T(8,128)(2,1)} %param.5) | data formatting | bytes 20447232 | tf_op args[1]
  21.5 30.0 %all-gather.6.cloned.1.call-done = bf16[1,512,1664]{2,1,0:T(8,128)(2,1)} async-done(((bf16[1,128,1664]{2,1,0:T(8,128)(2,1)}), bf16[1,512,1664]{2,1,0:T(8,128)(2,1)}) %all-gather.6.cloned.1.call-update) | async-done | bytes 1703952 | tf_op jit(solution)/shard_map/all_gather | solution.py:57
  51.5 9.1 %fusion.2 = f32[512,3072]{1,0:T(8,128)S(1)} fusion(bf16[1664,3072]{0,1:T(8,128)(2,1)} %bitcast.57, bf16[1,512,1664]{2,1,0:T(8,128)(2,1)} %all-gather.6.cloned.1.call-done), kind=kOutput, calls=%fused_computation.7 | convolution fusion | flops 5234491392 | bytes 18219008 | tf_op jit(solution)/shard_map/dot_general | solution.py:56
  60.6 2.7 %copy-done.1 = f32[512,3072]{1,0:T(8,128)} copy-done((f32[512,3072]{1,0:T(8,128)}, f32[512,3072]{1,0:T(8,128)S(1)}, u32[]{:S(2)}) %copy-start.1) | copy-done | bytes 6291480
  63.3 2.5 %slice.30 = f32[512,2048]{1,0:T(8,128)} slice(f32[512,3072]{1,0:T(8,128)S(1)} %fusion.2), slice={[0:512], [1024:3072]} | slice | bytes 8388608 | tf_op jit(solution)/shard_map/slice | solution.py:64
  65.9 51.5 %reduce-scatter.3.cloned.1.call-done = f32[128,2048]{1,0:T(8,128)} async-done(((f32[512,2048]{1,0:T(8,128)}), f32[128,2048]{1,0:T(8,128)}) %reduce-scatter.3.cloned.1.call-update) | async-done | bytes 1048592 | tf_op jit(solution)/shard_map/reduce_scatter | solution.py:69
  117.4 2.1 %convert_element_type.29 = bf16[128,2048]{1,0:T(8,128)(2,1)} convert(f32[128,2048]{1,0:T(8,128)} %reduce-scatter.3.cloned.1.call-done) | non-fusion elementwise | flops 262144 | bytes 1572864 | tf_op jit(solution)/shard_map/convert_element_type | solution.py:69
  119.6 3.2 %slice.32 = f32[512,1024]{1,0:T(8,128)} slice(f32[512,3072]{1,0:T(8,128)} %copy-done.1), slice={[0:512], [0:1024]} | slice | bytes 4194304 | tf_op jit(solution)/shard_map/slice | solution.py:63
  122.8 3.5 %gather_fusion = s32[512]{0:T(512)S(1)} fusion(s32[512]{0:T(512)S(1)} %bitcast.55, s32[1024]{0:T(1024)S(1)} %pad_clamp_fusion.1), kind=kCustom, calls=%fused_computation | custom fusion | bytes 6144 | tf_op jit(solution)/shard_map/jit(_take)/gather | solution.py:22
  126.4 1.3 gather_fusion.1
  127.7 0.7 fusion.31
  128.3 2.6 %fusion.28 = pred[128]{0:T(512)(128)(4,1)S(1)} fusion(s32[]{:T(128)} %bitcast, s32[]{:T(128)} %bitcast.1, s32[]{:T(128)} %bitcast.3, s32[]{:T(128)} %bitcast.2, s32[]{:T(128)S(6)} %mul.9), kind=kLoop, calls=%fused_computation.48 | loop fusion | flops 6272 | bytes 148 | tf_op jit(solution)/shard_map/eq | solution.py:67
  131.0 23.8 %all-gather.4.cloned.1.call-done = bf16[512,2048]{1,0:T(8,128)(2,1)} async-done(((bf16[128,2048]{1,0:T(8,128)(2,1)}), bf16[512,2048]{1,0:T(8,128)(2,1)}) %all-gather.4.cloned.1.call-update) | async-done | bytes 2097168 | tf_op jit(solution)/shard_map/all_gather | solution.py:72
  154.9 1.7 slice_bitcast_fusion
  156.6 0.5 copy.17
  157.2 35.7 %reduce-scatter.5.cloned.1.call-done = f32[128,1024]{1,0:T(8,128)} async-done(((f32[512,1024]{1,0:T(8,128)}), f32[128,1024]{1,0:T(8,128)}) %reduce-scatter.5.cloned.1.call-update) | async-done | bytes 524304 | tf_op jit(solution)/shard_map/reduce_scatter | solution.py:68
  192.9 3.3 %fusion.32 = (f32[8,128]{1,0:T(8,128)S(1)}, f32[8,128,512]{2,1,0:T(8,128)}) fusion(pred[128,512]{1,0:T(8,128)(4,1)S(1)} %fusion.12, bf16[64,8,8,128]{3,2,1,0:T(8,128)(2,1)S(1)} %get-tuple-element.2, f32[128,1024]{1,0:T(8,128)} %reduce-scatter.5.cloned.1.call-done), kind=kOutput, calls=%fused_computation.53 | convolution fusion | flops 136446464 | bytes 3739648 | tf_op jit(solution)/shard_map/sub | solution.py:40
  196.2 2.2 %convolution_convert_fusion = bf16[8,128,128]{2,1,0:T(8,128)(2,1)S(1)} fusion(bf16[512,8,128]{0,2,1:T(8,128)(2,1)S(1)} %bitcast.58, f32[8,128,512]{2,1,0:T(8,128)} %get-tuple-element.9, f32[8,128]{1,0:T(8,128)S(1)} %get-tuple-element.8), kind=kOutput, calls=%fused_computation.9 | convolution fusion | flops 135397376 | bytes 3411968 | tf_op jit(solution)/shard_map/hrs,shd->rhd/dot_general | solution.py:42
  198.4 0.1 copy.16
  198.7 0.1 copy.15
  198.9 0.8 broadcast_select_fusion.1
  199.7 0.6 collective-permute-done
  200.2 0.7 copy.45
  (21 shorter events, 0.5 us)
Async XLA Ops:
  7.2 115.7 %copy-start = (s32[1,512]{1,0:T(1,128)S(1)}, s32[1,512]{1,0:T(1,128)}, u32[]{:S(2)}) copy-start(s32[1,512]{1,0:T(1,128)} %param.6) | copy-start | bytes 6148
  7.2 44.3 %all-gather.6.cloned.1.call-start = ((), (), s32[]{:S(2)}) async-start(), calls=%async_computation.5 | async-start | bytes 2129920 | tf_op jit(solution)/shard_map/all_gather | solution.py:57
  7.9 109.5 %reduce-scatter.3.cloned.1.call-start = ((), (), s32[]{:S(2)}) async-start(), calls=%async_computation.2 | async-start | bytes 5242880 | tf_op jit(solution)/shard_map/reduce_scatter | solution.py:69
  60.6 2.7 %copy-start.1 = (f32[512,3072]{1,0:T(8,128)}, f32[512,3072]{1,0:T(8,128)S(1)}, u32[]{:S(2)}) copy-start(f32[512,3072]{1,0:T(8,128)S(1)} %fusion.2) | copy-start | bytes 18874372
  65.8 89.1 %all-gather.4.cloned.1.call-start = ((), (), s32[]{:S(2)}) async-start(), calls=%async_computation.3 | async-start | bytes 2621440 | tf_op jit(solution)/shard_map/all_gather | solution.py:72
  119.5 73.4 %reduce-scatter.5.cloned.1.call-start = ((), (), s32[]{:S(2)}) async-start(), calls=%async_computation.4 | async-start | bytes 2621440 | tf_op jit(solution)/shard_map/reduce_scatter | solution.py:68
  122.8 4.9 %copy-start.2 = (s32[1,4]{1,0:T(1,128)S(1)}, s32[1,4]{1,0:T(1,128)}, u32[]{:S(2)}) copy-start(s32[1,4]{1,0:T(1,128)} %param.7) | copy-start | bytes 52
  198.6 1.6 collective-permute-start
Sparse Core Ops, SparseCore 0:
  9.6 41.8 all-gather.5
  65.9 51.4 reduce-scatter.2
  119.6 35.1 all-gather.3
  157.7 35.1 reduce-scatter.4
where the time goes:
time: 208 us; the launch traced here: 207 us
  waiting for transfers between devices  142 us (68%)
  local copies, waits for them, and re-layouts  30.7 us (15%)
  matrix products  14.6 us (7%)
  between operations  13.9 us (7%)
  other arithmetic  5.68 us (3%)
    reduce_scatter x1, waiting for transfers between devices, local(): lax.psum_scatter(key_value_part, 'mp', scatter_dimension=0, tiled=True)  51.5 us
    reduce_scatter x1, waiting for transfers between devices, local(): lax.psum_scatter(query_part, 'mp', scatter_dimension=0, tiled=True)  35.7 us
    all_gather x1, waiting for transfers between devices, local(): lax.all_gather(rows_here, 'tok', axis=0, tiled=True)  30 us
    all_gather x1, waiting for transfers between devices, local(): key_value = lax.all_gather(mine, 'mp', axis=0, tiled=True)  23.8 us
    unnamed x9, local copies, waits for them, and re-layouts  18.7 us
    dot_general x1, matrix products, local(): jnp.dot(lax.all_gather(rows_here, 'tok', axis=0, tiled=True), flat_weight...  9.08 us
  transfers between devices with their start and end apart: 5, of which 5 were waited for; matrix products, arithmetic and copies ran while one was open for 14% of the time, Pallas kernels for 0%

commit v1 on v0

--- a/solution.py
+++ b/solution.py
@@ -6,6 +6,17 @@
 
 HEAD = 128
 BLOCK = 128
+
+
+def gather_by_hops(x, mesh_axis, d):
+    count = lax.axis_size(mesh_axis)
+    route = [(i, (i + 1) % count) for i in range(count)]
+    pieces = [x]
+    for far in range(1, count):
+        pieces = [lax.ppermute(pieces[0], mesh_axis, route), *pieces]
+    whole = jnp.concatenate(pieces, axis=d)
+    turn = (lax.axis_index(mesh_axis) + 1) * pieces[-1].shape[d]
+    return jnp.roll(whole, turn, axis=d)
 
 
 def shifted(block, axis, distance):
@@ -69,7 +80,7 @@
     mine = lax.psum_scatter(key_value_part, "mp", scatter_dimension=0, tiled=True).astype(
         jnp.bfloat16
     )
-    key_value = lax.all_gather(mine, "mp", axis=0, tiled=True)
+    key_value = gather_by_hops(mine, "mp", 0)
     all_pos = jnp.arange(total, dtype=jnp.int32)
     mixed = attend(
         query, key_value[:, :head_cols], key_value[:, head_cols:], my_pos, segment, all_pos

time: 208 us -> 191 us (0.918)
  waiting for transfers between devices: 142 us -> 123 us
  starting transfers between devices: 0.23 us -> 4.3 us
    ppermute x0 -> x3, waiting for transfers between devices: none -> 43.5 us  [gather_by_hops(): pieces = [lax.ppermute(pieces[0], mesh_axis, route), *pieces]]
    reduce_scatter x1, waiting for transfers between devices: 35.7 us -> 0.02 us  [local(): lax.psum_scatter(query_part, 'mp', scatter_dimension=0, tiled=True)]
    all_gather x1 -> x0, waiting for transfers between devices: 23.8 us -> none  [local(): key_value = lax.all_gather(mine, 'mp', axis=0, tiled=True)]
    ppermute x0 -> x3, starting transfers between devices: none -> 4.12 us  [gather_by_hops(): pieces = [lax.ppermute(pieces[0], mesh_axis, route), *pieces]]
    reduce_scatter x1, waiting for transfers between devices: 51.5 us -> 48.3 us  [local(): lax.psum_scatter(key_value_part, 'mp', scatter_dimension=0, tiled=True)]
    unnamed x9 -> x17, local copies, waits for them, and re-layouts: 18.7 us -> 17.3 us
  transfers between devices with their start and end apart: 5 -> 7, of which waited for: 5 -> 6; matrix products, arithmetic and copies ran while one was open for 14% -> 15% of each run, Pallas kernels for 0% -> 0%
where the time goes in v1:
time: 191 us; the launch traced here: 190 us
  waiting for transfers between devices  123 us (64%)
  local copies, waits for them, and re-layouts  29.2 us (15%)
  matrix products  14.6 us (8%)
  between operations  14 us (7%)
  other arithmetic  5.09 us (3%)
  starting transfers between devices  4.3 us (2%)
    reduce_scatter x1, waiting for transfers between devices, local(): lax.psum_scatter(key_value_part, 'mp', scatter_dimension=0, tiled=True)  48.3 us
    ppermute x3, waiting for transfers between devices, gather_by_hops(): pieces = [lax.ppermute(pieces[0], mesh_axis, route), *pieces]  43.5 us
    all_gather x1, waiting for transfers between devices, local(): lax.all_gather(rows_here, 'tok', axis=0, tiled=True)  30.1 us
    unnamed x17, local copies, waits for them, and re-layouts  17.3 us
    dot_general x1, matrix products, local(): jnp.dot(lax.all_gather(rows_here, 'tok', axis=0, tiled=True), flat_weight...  9.08 us
    ppermute x3, starting transfers between devices, gather_by_hops(): pieces = [lax.ppermute(pieces[0], mesh_axis, route), *pieces]  4.12 us
  transfers between devices with their start and end apart: 7, of which 6 were waited for; matrix products, arithmetic and copies ran while one was open for 15% of the time, Pallas kernels for 0%

profile of v1, /device:TPU:0, one launch (start us, length us, event | category | flops | bytes accessed | tf_op | source)
XLA Modules:
  0.0 190.4 jit_solution(2997901641505146020)
XLA Ops:
  7.2 0.7 all-gather.3.cloned.1.call-update
  8.0 13.5 %copy.11 = bf16[1,1664,3,1024]{1,3,2,0:T(8,128)(2,1)} copy(bf16[1,1664,3,1024]{3,1,2,0:T(8,128)(2,1)} %param.5) | data formatting | bytes 20447232 | tf_op args[1]
  21.4 30.1 %all-gather.3.cloned.1.call-done = bf16[1,512,1664]{2,1,0:T(8,128)(2,1)} async-done(((bf16[1,128,1664]{2,1,0:T(8,128)(2,1)}), bf16[1,512,1664]{2,1,0:T(8,128)(2,1)}) %all-gather.3.cloned.1.call-update) | async-done | bytes 1703952 | tf_op jit(solution)/shard_map/all_gather | solution.py:68
  51.5 9.1 %fusion.2 = f32[512,3072]{1,0:T(8,128)S(1)} fusion(bf16[1664,3072]{0,1:T(8,128)(2,1)} %bitcast.57, bf16[1,512,1664]{2,1,0:T(8,128)(2,1)} %all-gather.3.cloned.1.call-done), kind=kOutput, calls=%fused_computation.7 | convolution fusion | flops 5234491392 | bytes 18219008 | tf_op jit(solution)/shard_map/dot_general | solution.py:67
  60.6 2.7 %copy-done.2 = f32[512,3072]{1,0:T(8,128)} copy-done((f32[512,3072]{1,0:T(8,128)}, f32[512,3072]{1,0:T(8,128)S(1)}, u32[]{:S(2)}) %copy-start.2) | copy-done | bytes 6291480
  63.2 2.5 %slice.30 = f32[512,2048]{1,0:T(8,128)} slice(f32[512,3072]{1,0:T(8,128)S(1)} %fusion.2), slice={[0:512], [1024:3072]} | slice | bytes 8388608 | tf_op jit(solution)/shard_map/slice | solution.py:75
  65.8 3.2 %slice.31 = f32[512,1024]{1,0:T(8,128)} slice(f32[512,3072]{1,0:T(8,128)} %copy-done.2), slice={[0:512], [0:1024]} | slice | bytes 4194304 | tf_op jit(solution)/shard_map/slice | solution.py:74
  69.0 48.3 %reduce-scatter.3.cloned.1.call-done = f32[128,2048]{1,0:T(8,128)} async-done(((f32[512,2048]{1,0:T(8,128)}), f32[128,2048]{1,0:T(8,128)}) %reduce-scatter.3.cloned.1.call-update) | async-done | bytes 1048592 | tf_op jit(solution)/shard_map/reduce_scatter | solution.py:80
  117.4 1.4 convert_element_type.29
  118.8 1.5 collective-permute-start
  120.3 17.7 %collective-permute-done = bf16[128,2048]{1,0:T(8,128)(2,1)S(1)} collective-permute-done((bf16[128,2048]{1,0:T(8,128)(2,1)S(1)}, bf16[128,2048]{1,0:T(8,128)(2,1)S(1)}, u32[]{:S(2)}, u32[]{:S(2)}) %collective-permute-start) | collective-permute-done | bytes 524320 | tf_op jit(solution)/shard_map/ppermute | solution.py:16
  137.9 2.0 %collective-permute-start.1 = (bf16[128,2048]{1,0:T(8,128)(2,1)S(1)}, bf16[128,2048]{1,0:T(8,128)(2,1)S(1)}, u32[]{:S(2)}, u32[]{:S(2)}) collective-permute-start(bf16[128,2048]{1,0:T(8,128)(2,1)S(1)} %collective-permute-done), channel_id=1, source_target_pairs={{0,1},{1,2},{2,3},{3,0},{4,5},{5,6},{6,7},{7,4},{8,9},{9,10},{10,1... | collective-permute-start | bytes 1572872 | tf_op jit(solution)/shard_map/ppermute | solution.py:16
  140.0 3.5 %gather_fusion = s32[512]{0:T(512)S(1)} fusion(s32[512]{0:T(512)S(1)} %bitcast.55, s32[1024]{0:T(1024)S(1)} %get-tuple-element.11), kind=kCustom, calls=%fused_computation | custom fusion | bytes 6144 | tf_op jit(solution)/shard_map/jit(_take)/gather | solution.py:33
  143.5 1.3 gather_fusion.1
  144.8 0.6 fusion.31
  145.5 10.2 %collective-permute-done.1 = bf16[128,2048]{1,0:T(8,128)(2,1)S(1)} collective-permute-done((bf16[128,2048]{1,0:T(8,128)(2,1)S(1)}, bf16[128,2048]{1,0:T(8,128)(2,1)S(1)}, u32[]{:S(2)}, u32[]{:S(2)}) %collective-permute-start.1) | collective-permute-done | bytes 524320 | tf_op jit(solution)/shard_map/ppermute | solution.py:16
  155.7 0.6 collective-permute-start.2
  156.3 2.6 %fusion.28 = pred[128]{0:T(512)(128)(4,1)S(1)} fusion(s32[]{:T(128)} %bitcast, s32[]{:T(128)} %bitcast.1, s32[]{:T(128)} %bitcast.3, s32[]{:T(128)} %bitcast.2, s32[]{:T(128)S(6)} %mul.12), kind=kLoop, calls=%fused_computation.56 | loop fusion | flops 6272 | bytes 148 | tf_op jit(solution)/shard_map/eq | solution.py:78
  159.0 15.6 %collective-permute-done.2 = bf16[128,2048]{1,0:T(8,128)(2,1)S(1)} collective-permute-done((bf16[128,2048]{1,0:T(8,128)(2,1)S(1)}, bf16[128,2048]{1,0:T(8,128)(2,1)S(1)}, u32[]{:S(2)}, u32[]{:S(2)}) %collective-permute-start.2) | collective-permute-done | bytes 524320 | tf_op jit(solution)/shard_map/ppermute | solution.py:16
  175.8 3.3 %fusion.32 = (f32[8,128]{1,0:T(8,128)S(1)}, f32[8,128,512]{2,1,0:T(8,128)}) fusion(pred[128,512]{1,0:T(8,128)(4,1)S(1)} %fusion.12, bf16[64,8,8,128]{3,2,1,0:T(8,128)(2,1)S(1)} %get-tuple-element.2, f32[128,1024]{1,0:T(8,128)} %reduce-scatter.5.cloned.1.call-done), kind=kOutput, calls=%fused_computation.61 | convolution fusion | flops 136446464 | bytes 3739648 | tf_op jit(solution)/shard_map/sub | solution.py:51
  179.1 2.2 %convolution_convert_fusion = bf16[8,128,128]{2,1,0:T(8,128)(2,1)S(1)} fusion(bf16[512,8,128]{0,2,1:T(8,128)(2,1)S(1)} %bitcast.58, f32[8,128,512]{2,1,0:T(8,128)} %get-tuple-element.9, f32[8,128]{1,0:T(8,128)S(1)} %get-tuple-element.8), kind=kOutput, calls=%fused_computation.9 | convolution fusion | flops 135397376 | bytes 3411968 | tf_op jit(solution)/shard_map/hrs,shd->rhd/dot_general | solution.py:53
  181.8 0.8 broadcast_select_fusion.1
  182.6 0.6 collective-permute-done.3
  183.2 0.7 copy.52
  (34 shorter events, 1.9 us)
Async XLA Ops:
  7.2 132.8 %copy-start = (s32[1,512]{1,0:T(1,128)S(1)}, s32[1,512]{1,0:T(1,128)}, u32[]{:S(2)}) copy-start(s32[1,512]{1,0:T(1,128)} %param.6) | copy-start | bytes 6148
  7.2 44.3 %all-gather.3.cloned.1.call-start = ((), (), s32[]{:S(2)}) async-start(), calls=%async_computation.4 | async-start | bytes 2129920 | tf_op jit(solution)/shard_map/all_gather | solution.py:68
  7.9 109.5 %reduce-scatter.3.cloned.1.call-start = ((), (), s32[]{:S(2)}) async-start(), calls=%async_computation.2 | async-start | bytes 5242880 | tf_op jit(solution)/shard_map/reduce_scatter | solution.py:80
  60.6 2.7 %copy-start.2 = (f32[512,3072]{1,0:T(8,128)}, f32[512,3072]{1,0:T(8,128)S(1)}, u32[]{:S(2)}) copy-start(f32[512,3072]{1,0:T(8,128)S(1)} %fusion.2) | copy-start | bytes 18874372
  65.8 110.0 %reduce-scatter.5.cloned.1.call-start = ((), (), s32[]{:S(2)}) async-start(), calls=%async_computation.3 | async-start | bytes 2621440 | tf_op jit(solution)/shard_map/reduce_scatter | solution.py:79
  69.0 75.8 %copy-start.3 = (s32[1,4]{1,0:T(1,128)S(1)}, s32[1,4]{1,0:T(1,128)}, u32[]{:S(2)}) copy-start(s32[1,4]{1,0:T(1,128)} %param.7) | copy-start | bytes 52
  117.4 57.3 %copy-start.1 = (f32[128,2048]{1,0:T(8,128)S(1)}, f32[128,2048]{1,0:T(8,128)}, u32[]{:S(2)}) copy-start(f32[128,2048]{1,0:T(8,128)} %reduce-scatter.3.cloned.1.call-done) | copy-start | bytes 3145732
  118.8 19.2 %collective-permute-start = (bf16[128,2048]{1,0:T(8,128)(2,1)S(1)}, bf16[128,2048]{1,0:T(8,128)(2,1)S(1)}, u32[]{:S(2)}, u32[]{:S(2)}) collective-permute-start(bf16[128,2048]{1,0:T(8,128)(2,1)S(1)} %convert_element_type.29), channel_id=1, source_target_pairs={{0,1},{1,2},{2,3},{3,0},{4,5},{5,6},{6,7},{7,4},{8,9},{9,10},{10,1... | collective-permute-start | bytes 1572872 | tf_op jit(solution)/shard_map/ppermute | solution.py:16
  137.9 17.8 %collective-permute-start.1 = (bf16[128,2048]{1,0:T(8,128)(2,1)S(1)}, bf16[128,2048]{1,0:T(8,128)(2,1)S(1)}, u32[]{:S(2)}, u32[]{:S(2)}) collective-permute-start(bf16[128,2048]{1,0:T(8,128)(2,1)S(1)} %collective-permute-done), channel_id=1, source_target_pairs={{0,1},{1,2},{2,3},{3,0},{4,5},{5,6},{6,7},{7,4},{8,9},{9,10},{10,1... | collective-permute-start | bytes 1572872 | tf_op jit(solution)/shard_map/ppermute | solution.py:16
  155.7 18.9 %collective-permute-start.2 = (bf16[128,2048]{1,0:T(8,128)(2,1)S(1)}, bf16[128,2048]{1,0:T(8,128)(2,1)S(1)}, u32[]{:S(2)}, u32[]{:S(2)}) collective-permute-start(bf16[128,2048]{1,0:T(8,128)(2,1)S(1)} %collective-permute-done.1), channel_id=1, source_target_pairs={{0,1},{1,2},{2,3},{3,0},{4,5},{5,6},{6,7},{7,4},{8,9},{9,10},{10,1... | collective-permute-start | bytes 1572872 | tf_op jit(solution)/shard_map/ppermute | solution.py:16
  181.6 1.6 collective-permute-start.3
Sparse Core Ops, SparseCore 0:
  9.6 41.8 all-gather.2
  65.9 51.4 reduce-scatter.2
  120.4 49.0 reduce-scatter.4
